TPU v7x, 512 devices: a whole 4x4x16 slice. The times are simulated.
512 devices in a mesh: occ: 16 (over x, z_hi), aux: 32 (over z_lo, y, core).
Axes of the slice: x: 4, y: 4, z: 16 (z_hi: 4, z_lo: 4; z = z_hi * 4 + z_lo), core: 2. Of those that a mesh axis runs over, the one named last changes fastest.
Arguments:
- integrals: bfloat16 [16384, 64, 256], P(('aux', 'occ')), may hold values from -0.59765625 to 0.59765625
- eps_occ: float32 [1024], replicated, may hold values from -3 to -0.5
- eps_vir: float32 [4096], replicated, may hold values from 0.5 to 4
- src_occ: int32 [4], replicated, may hold values from 0 to 63
- occ_offset: int32 [1], replicated, may hold values from 0 to 960
- vir_offset: int32 [1], replicated, may hold values from 0 to 3840
Outputs:
- density: bfloat16 [16384, 64, 256], P('aux', 'occ')
Inputs may be any that keep to these rules, and one draw needn't show every extreme that they name: `src_occ`: each entry is an occupied index inside the window. `occ_offset`: the window of 64 occupied orbitals lies inside the occupied energies. `vir_offset`: the block of 256 virtual orbitals lies inside the virtual energies.
All inputs are finite; a program needn't handle non-finite values.
Results may differ from a plain program's by a relative error of at most 0.009.
Values may be sent and summed in bfloat16 or wider, within the bound.
A program may use at most 64 MiB of HBM per device.

v0:
```python
import jax
import jax.numpy as jnp
from jax import lax
from jax.sharding import PartitionSpec as P

NSRC = 4


def spread(value, axis, source):
    kept = jnp.where(lax.axis_index(axis) == source, value, 0).astype(value.dtype)
    return lax.psum(kept, axis)


def local(integrals, eps_occ, eps_vir, src_occ, occ_offset, vir_offset):
    owned_ints = lax.all_to_all(integrals, "occ", split_axis=1, concat_axis=0, tiled=True)
    aux_rows, occ_count, virt_count = owned_ints.shape
    my_occ = lax.axis_index("occ")
    occ_energy = lax.dynamic_slice_in_dim(eps_occ, occ_offset[0] + my_occ * occ_count, occ_count)
    vir_energy = lax.dynamic_slice_in_dim(eps_vir, vir_offset[0], virt_count)
    flat_ints = owned_ints.reshape(aux_rows, occ_count * virt_count)
    local_index = src_occ % occ_count
    owner_index = src_occ // occ_count
    density_sum = jnp.zeros((aux_rows, occ_count * virt_count), jnp.float32)
    for source_step in range(NSRC):
        candidate = lax.dynamic_index_in_dim(
            owned_ints, local_index[source_step], 1, keepdims=False
        )
        source = spread(candidate, "occ", owner_index[source_step])
        partial_value = lax.dot_general(
            flat_ints, source, (((0,), (0,)), ((), ())), preferred_element_type=jnp.float32
        )
        partial_value = partial_value.reshape(occ_count, virt_count, virt_count)
        src_energy = lax.dynamic_index_in_dim(
            eps_occ, occ_offset[0] + src_occ[source_step], 0, keepdims=False
        )
        pair_sum = lax.psum(partial_value, "aux")
        denom = (
            vir_energy[None, :, None]
            + vir_energy[None, None, :]
            - occ_energy[:, None, None]
            - src_energy
        )
        scaled = (pair_sum / denom).astype(jnp.bfloat16)
        scaled_wide = scaled.astype(jnp.float32)
        amplitude = (2.0 * scaled_wide - jnp.transpose(scaled_wide, (0, 2, 1))).astype(jnp.bfloat16)
        density_sum = density_sum + lax.dot_general(
            source,
            amplitude.reshape(occ_count * virt_count, virt_count),
            (((1,), (1,)), ((), ())),
            preferred_element_type=jnp.float32,
        )
    return density_sum.astype(jnp.bfloat16).reshape(aux_rows, occ_count, virt_count)


def solution(mesh):
    in_specs = (P(("aux", "occ"), None, None), P(), P(), P(), P(), P())
    out_specs = P("aux", "occ", None)
    return jax.shard_map(local, mesh=mesh, in_specs=in_specs, out_specs=out_specs, check_vma=False)
```

profile of v0, /device:TPU:1, one launch (start us, length us, event | category | flops | bytes accessed | tf_op | source)
XLA Modules:
  0.0 640.4 jit_solution(16349789741271124798)
XLA Ops:
  6.5 2.8 copy.24
  9.3 18.2 %all-to-all-start = ((bf16[32,64,256]{2,0,1:T(8,128)(2,1)}), bf16[32,64,256]{2,0,1:T(8,128)(2,1)S(1)}, u32[]{:S(2)}, u32[]{:S(2)}) async-start(bf16[32,64,256]{2,0,1:T(8,128)(2,1)} %copy.24), calls=%async_computation | async-start | bytes 2097152 | tf_op jit(solution)/shard_map/all_to_all | solution.py:15
  27.5 0.0 all-reduce.7.cloned.1.call-start
  27.6 0.7 fusion.18
  38.4 38.6 %all-to-all-done = bf16[32,64,256]{2,0,1:T(8,128)(2,1)S(1)} async-done(((bf16[32,64,256]{2,0,1:T(8,128)(2,1)}), bf16[32,64,256]{2,0,1:T(8,128)(2,1)S(1)}, u32[]{:S(2)}, u32[]{:S(2)}) %all-to-all-start) | async-done | bytes 1048608 | tf_op jit(solution)/shard_map/all_to_all | solution.py:15
  77.0 0.1 copy.25
  77.1 1.0 select_bitcast_fusion
  78.1 0.0 all-reduce.7.cloned.1.call-update
  78.1 0.0 all-reduce.5.cloned.1.call-start
  78.2 0.9 copy.26
  79.0 0.2 copy.43
  79.3 203.8 %all-reduce.7.cloned.1.call-done = (bf16[512,256]{1,0:T(8,128)(2,1)}, bf16[512,256]{1,0:T(8,128)(2,1)}, bf16[512,256]{1,0:T(8,128)(2,1)}, bf16[512,256]{1,0:T(8,128)(2,1)}) async-done(((bf16[512,256]{1,0:T(8,128)(2,1)}, bf16[512,256]{1,0:T(8,128)(2,1)}, bf16[512,256]{1,0:T(8,128)(2,1)}, bf16[512,256]{1,0:T(8,128)(2,1)}), (bf16[512,256]{1,0:T(8,128)(2,1)}, bf16[512,256]{1,0:T(8,128)(2,1)}, ...) | async-done | bytes 1048592 | tf_op jit(solution)/shard_map/psum | solution.py:11
  283.1 1.4 convolution_bitcast_fusion.2
  284.5 1.3 copy.40
  285.8 0.5 convolution_bitcast_fusion
  286.3 1.3 copy.42
  287.6 0.5 convolution_bitcast_fusion.3
  288.1 1.3 copy.39
  289.4 0.5 convolution_bitcast_fusion.1
  289.9 1.3 copy.41
  291.2 0.0 all-reduce.5.cloned.1.call-update
  291.8 0.7 fusion.17
  295.8 0.1 dynamic_slice.34
  295.8 0.8 dynamic_slice.33
  296.6 0.7 fusion.16
  297.3 0.8 broadcast_add_fusion
  298.1 300.2 %all-reduce.5.cloned.1.call-done = (f32[4,256,256]{2,1,0:T(8,128)}, f32[4,256,256]{2,1,0:T(8,128)}, f32[4,256,256]{2,1,0:T(8,128)}, f32[4,256,256]{2,1,0:T(8,128)}) async-done(((f32[4,256,256]{2,1,0:T(8,128)}, f32[4,256,256]{2,1,0:T(8,128)}, f32[4,256,256]{2,1,0:T(8,128)}, f32[4,256,256]{2,1,0:T(8,128)}), (f32[4,256,256]{2,1,0:T(8,128)}, f32[4,256,256]{2,1,0:T(8,128)}, f32[4,256,256]{2,1,0:T(8,128)}, ...) | async-done | bytes 4194320 | tf_op jit(solution)/shard_map/psum | solution.py:36
  598.2 6.2 fusion.13
  604.4 1.3 copy.37
  605.7 2.2 fusion.10
  607.9 2.0 copy.38
  609.9 0.3 copy.31
  610.3 0.9 fusion.12
  611.2 2.0 copy.32
  613.3 1.6 fusion.21
  614.8 2.1 copy.28
  616.9 2.1 convert_multiply_fusion
  619.0 2.6 copy.29
  621.6 1.5 fusion.1
  623.1 1.8 fusion.20
  624.9 1.3 copy.34
  626.2 2.2 fusion.11
  628.4 1.2 copy.35
  629.6 1.6 fusion.22
  631.2 0.1 copy-done
  631.3 0.1 copy-done.1
  631.4 0.6 add_convert_fusion
  632.0 1.6 reshape.85
  (15 shorter events, 0.0 us)
Async XLA Ops:
  6.5 21.0 %copy-start.6 = (s32[4]{0:T(128)S(1)}, s32[4]{0:T(128)}, u32[]{:S(2)}) copy-start(s32[4]{0:T(128)} %param.9) | copy-start | bytes 52
  9.3 67.7 %all-to-all-start = ((bf16[32,64,256]{2,0,1:T(8,128)(2,1)}), bf16[32,64,256]{2,0,1:T(8,128)(2,1)S(1)}, u32[]{:S(2)}, u32[]{:S(2)}) async-start(bf16[32,64,256]{2,0,1:T(8,128)(2,1)} %copy.24), calls=%async_computation | async-start | bytes 2097152 | tf_op jit(solution)/shard_map/all_to_all | solution.py:15
  27.5 255.5 %all-reduce.7.cloned.1.call-start = ((), (), s32[]{:S(2)}) async-start(), calls=%async_computation.2 | async-start | bytes 2097152 | tf_op jit(solution)/shard_map/psum | solution.py:11
  78.1 520.1 %all-reduce.5.cloned.1.call-start = ((), (), s32[]{:S(2)}) async-start(), calls=%async_computation.1 | async-start | bytes 8388608 | tf_op jit(solution)/shard_map/psum | solution.py:36
  283.1 2.8 copy-start.2
  285.8 1.8 copy-start.4
  287.6 1.8 copy-start.3
  291.2 4.6 copy-start.7
  621.6 1.5 copy-start.5
  629.6 1.7 copy-start
  629.6 1.7 copy-start.1
Sparse Core Ops, SparseCore 0:
  78.2 204.7 all-reduce.6
  291.3 306.8 all-reduce.4
where the time goes:
time: 641 us; the launch traced here: 640 us
  waiting for transfers between devices  543 us (85%)
  between operations  27.5 us (4%)
  local copies, waits for them, and re-layouts  26.8 us (4%)
  starting transfers between devices  18.3 us (3%)
  other arithmetic  16.9 us (3%)
  matrix products  8.38 us (1%)
    psum x1, waiting for transfers between devices, local(): pair_sum = lax.psum(partial_value, 'aux')  300 us
    psum x1, waiting for transfers between devices, spread(): return lax.psum(kept, axis)  204 us
    all_to_all x1, waiting for transfers between devices, local(): lax.all_to_all(integrals, 'occ', split_axis=1, concat_axis=0, tiled=True)  38.6 us
    all_to_all x1, starting transfers between devices, local(): lax.all_to_all(integrals, 'occ', split_axis=1, concat_axis=0, tiled=True)  18.2 us
  transfers between devices with their start and end apart: 3, of which 3 were waited for; matrix products, arithmetic and copies ran while one was open for 1% of the time, Pallas kernels for 0%

commit v1 on v0

v1 whole, which is shorter than its diff:
```python
import jax
import jax.numpy as jnp
from jax import lax
from jax.experimental import pallas as pl
from jax.experimental.pallas import tpu as pltpu
from jax.sharding import PartitionSpec as P

MESH = pl.DeviceIdType.MESH
F32, BF16 = jnp.float32, jnp.bfloat16


def coords():
    occ, aux = lax.axis_index("occ"), lax.axis_index("aux")
    return occ // 4, (aux // 2) % 4, (occ % 4) * 4 + aux // 8, aux % 2


def device(x, y, z, c):
    return {"occ": x * 4 + z // 4, "aux": ((z % 4) * 4 + y) * 2 + c}


A0, SRC1, SRC2, FWD, ZG, XG, RING, XCH, AZ, AY, AC, LOCAL, COUNT = (
    0, 32, 38, 44, 52, 55, 58, 90, 91, 94, 106, 122, 125,
)
ORDER = (1, 3, 2)


def kernel(a_ref, s_ref, den_ref, d_ref, ar, at, sr, sd, cc, rb, sb, s16, xb, amp, dacc, snd, rcv):
    x, y, z, c = coords()
    zh, zl = z // 4, z % 4

    def copy(src, dst, slot, dev):
        return pltpu.make_async_remote_copy(
            src_ref=src, dst_ref=dst, send_sem=snd.at[slot], recv_sem=rcv.at[slot],
            device_id=dev, device_id_type=MESH,
        )

    barrier = pltpu.get_barrier_semaphore()

    def greet(dev):
        pl.semaphore_signal(barrier, inc=1, device_id=dev, device_id_type=MESH)

    def plane(o):
        return device((x + o // 8) % 4, (y + (o // 2) % 4) % 4, z, (c + o) % 2)

    @pl.loop(1, 32)
    def _(o):
        greet(plane(o))

    greet(device(x, y, (z + 1) % 16, c))
    greet(device(x, y, (z + 15) % 16, c))
    for j in (1, 2, 3):
        greet(device(x, y, (z + 4 * j) % 16, c))
        greet(device(x, y, zh * 4 + (zl + j) % 4, c))
    pl.semaphore_wait(barrier, 39)

    locals_ = [
        pltpu.make_async_copy(a_ref.at[x, :, y, c], ar.at[:, x, y, c], rcv.at[LOCAL]),
        pltpu.make_async_copy(s_ref, sr.at[:, x, y, c], rcv.at[LOCAL + 1]),
        pltpu.make_async_copy(s_ref, sd.at[:, x, zh], rcv.at[LOCAL + 2]),
    ]
    for cp in locals_:
        cp.start()

    xs = {j: (x + j) % 4 for j in (1, 2, 3)}
    ys = {j: (y + j) % 4 for j in (1, 2, 3)}
    first = [
        (copy(s_ref.at[0:2], sr.at[0:2, x, y, c], SRC1 + j - 1, device(xs[j], y, z, c)),
         copy(s_ref.at[2:4], sr.at[2:4, x, y, c], SRC1 + 2 + j, device(x, ys[j], z, c)))
        for j in ORDER
    ]
    for p, q in first:
        p.start()
        q.start()
    zg = [copy(s_ref, sd.at[:, x, zh], ZG + j - 1, device(x, y, (z + 4 * j) % 16, c)) for j in ORDER]
    for cp in zg:
        cp.start()

    def a_copy(o):
        tx, ty, tc = (x + o // 8) % 4, (y + (o // 2) % 4) % 4, (c + o) % 2
        return copy(a_ref.at[tx, :, ty, tc], ar.at[:, x, y, c], A0 + o, device(tx, ty, z, tc))

    @pl.loop(1, 32)
    def _(o):
        a_copy(o).start()

    for cp in locals_:
        cp.wait()
    other = device(x, y, z, 1 - c)
    fwd = []

    def forward(view, slot):
        cp = copy(view, view, slot, other)
        cp.start()
        fwd.append(cp)

    for p, q in first:
        p.wait_recv()
        q.wait_recv()
    vx, vy = sr.at[0:2, :, y, c], sr.at[2:4, x, :, c]
    second = []
    for j in ORDER:
        p = copy(vx, vx, SRC2 + j - 1, device(x, ys[j], z, c))
        q = copy(vy, vy, SRC2 + 2 + j, device(xs[j], y, z, c))
        p.start()
        q.start()
        second.append((p, q))
    forward(vx, FWD)
    forward(vy, FWD + 1)
    for n, j in enumerate(ORDER):
        p, q = second[n]
        p.wait_recv()
        forward(sr.at[0:2, :, (y + 4 - j) % 4, c], FWD + 2 + 2 * n)
        q.wait_recv()
        forward(sr.at[2:4, (x + 4 - j) % 4, :, c], FWD + 3 + 2 * n)

    @pl.loop(1, 32)
    def _(o):
        a_copy(o).wait_recv()

    @pl.loop(0, 4)
    def _(h):
        at[pl.ds(h * 128, 128), :] = ar[h].reshape(1024, 128).T

    for cp in zg:
        cp.wait_recv()
    vd = sd.at[:, x]
    xg = [copy(vd, vd, XG + j - 1, device(xs[j], y, z, c)) for j in ORDER]
    for cp in xg:
        cp.start()

    for cp in fwd:
        cp.wait_recv()

    @pl.loop(0, 4)
    def _(s):
        part = jnp.dot(at[...], sr[s].reshape(1024, 256), preferred_element_type=F32)
        for h in range(4):
            cc[h * 4 + s] = part[h * 128:(h + 1) * 128]

    up, down = device(x, y, (z + 1) % 16, c), device(x, y, (z + 15) % 16, c)

    def hop(way, d, q):
        return copy(sb.at[way, d - 1, q], rb.at[way, d - 1, q], RING + (way * 8 + d - 1) * 2 + q, up if way == 0 else down)

    def arrived(way, d, q):
        hop(way, d + 1, q).wait_recv()

    def send(way, d, q, add):
        target = (z + d) % 16 if way == 0 else (z + 16 - d) % 16
        value = cc[target, pl.ds(q * 64, 64), :]
        if add:
            arrived(way, d, q)
            value = value + rb[way, d, q].astype(F32)
        sb[way, d - 1, q] = value.astype(BF16)
        hop(way, d, q).start()

    for q in (0, 1):
        send(0, 8, q, False)
        send(1, 7, q, False)

    @pl.loop(1, 7)
    def _(k):
        for q in (0, 1):
            send(0, 8 - k, q, True)
            send(1, 7 - k, q, True)

    for q in (0, 1):
        send(0, 1, q, True)

    for q in (0, 1):
        rows = pl.ds(q * 64, 64)
        arrived(1, 0, q)
        total = cc[z, rows, :] + rb[1, 0, q].astype(F32)
        arrived(0, 0, q)
        total = total + rb[0, 0, q].astype(F32)
        s16[rows, :] = (total / den_ref[rows, :]).astype(BF16)

    mine, theirs = pl.ds(pl.multiple_of(c * 128, 128), 128), pl.ds(pl.multiple_of((1 - c) * 128, 128), 128)
    xch = copy(s16.at[:, theirs], xb, XCH, other)
    xch.start()
    own = amp.at[y * 4 + zl, c]
    s_mine = s16[:, mine].astype(F32)
    own[:, mine] = (2.0 * s_mine - s_mine.T).astype(BF16)
    xch.wait_recv()
    own[:, theirs] = (2.0 * s16[:, theirs].astype(F32) - xb[...].astype(F32).T).astype(BF16)

    def to_z(j):
        return copy(own, own, AZ + j - 1, device(x, y, zh * 4 + (zl + j) % 4, c))

    def block(j, m):
        return (y + 4 - m) % 4 * 4 + (zl + 4 - j) % 4

    def to_y(j, m):
        view = amp.at[block(j, 0), c]
        return copy(view, view, AY + j * 3 + m - 1, device(x, (y + m) % 4, z, c))

    def to_core(j, m):
        view = amp.at[block(j, m), c]
        return copy(view, view, AC + j * 4 + m, other)

    for j in ORDER:
        to_z(j).start()
    for j in (0, 1, 3, 2):
        if j:
            to_z(j).wait_recv()
        for m in ORDER:
            to_y(j, m).start()
        to_core(j, 0).start()
    for cp in xg:
        cp.wait_recv()

    def product(j, m):
        b = block(j, m)
        t, s = b // 4, b % 4
        to_core(j, m).wait_recv()
        return lax.dot_general(
            sd[s].reshape(512, 256), amp[b].reshape(256, 256), (((1,), (1,)), ((), ())), preferred_element_type=F32
        ), t

    for m in (0, 1, 3, 2):
        value, t = product(0, m) if m == 0 else (None, None)
        if m:
            to_y(0, m).wait_recv()
            to_core(0, m).start()
            value, t = product(0, m)
        dacc[t] = value

    for j in (1, 3, 2):
        for m in (0, 1, 3, 2):
            if m:
                to_y(j, m).wait_recv()
                to_core(j, m).start()
            value, t = product(j, m)
            if j == 2:
                d_ref[t] = (dacc[t] + value).astype(BF16)
            else:
                dacc[t] = dacc[t] + value

    @pl.loop(1, 32)
    def _(o):
        a_copy(o).wait_send()

    for p, q in first + second:
        p.wait_send()
        q.wait_send()
    for cp in zg + xg + fwd + [xch]:
        cp.wait_send()
    for q in (0, 1):
        hop(0, 8, q).wait_send()

        @pl.loop(1, 8)
        def _(d, q=q):
            hop(0, d, q).wait_send()
            hop(1, d, q).wait_send()

    for j in range(4):
        if j:
            to_z(j).wait_send()
        for m in range(4):
            if m:
                to_y(j, m).wait_send()
            to_core(j, m).wait_send()


def local(integrals, eps_occ, eps_vir, src_occ, occ_offset, vir_offset):
    x, y, z, c = coords()
    zh, zl = z // 4, z % 4
    ints = jnp.transpose(integrals, (1, 0, 2)).reshape(4, 4, 4, 32, 2, 128).transpose(0, 1, 2, 4, 3, 5)
    sources = jnp.stack([
        lax.dynamic_index_in_dim(integrals, src_occ[s], 1, keepdims=False) for s in range(4)
    ])
    vir = lax.dynamic_slice_in_dim(eps_vir, vir_offset[0], 256)
    vir_rows = lax.dynamic_slice_in_dim(vir, c * 128, 128)
    e_occ = lax.dynamic_index_in_dim(eps_occ, occ_offset[0] + (x * 4 + zh) * 4 + y, 0, keepdims=False)
    e_src = lax.dynamic_index_in_dim(
        eps_occ, occ_offset[0] + lax.dynamic_index_in_dim(src_occ, zl, 0, keepdims=False), 0, keepdims=False
    )
    denom = vir_rows[:, None] + vir[None, :] - e_occ - e_src
    vmem = pl.BlockSpec(memory_space=pltpu.VMEM)
    density = pl.pallas_call(
        kernel,
        out_shape=jax.ShapeDtypeStruct((4, 512, 256), BF16),
        in_specs=[vmem] * 3,
        out_specs=vmem,
        scratch_shapes=[
            pltpu.VMEM((4, 4, 4, 2, 32, 128), BF16),
            pltpu.VMEM((512, 1024), BF16),
            pltpu.VMEM((4, 4, 4, 2, 32, 256), BF16),
            pltpu.VMEM((4, 4, 4, 32, 256), BF16),
            pltpu.VMEM((16, 128, 256), F32),
            pltpu.VMEM((2, 8, 2, 64, 256), BF16),
            pltpu.VMEM((2, 8, 2, 64, 256), BF16),
            pltpu.VMEM((128, 256), BF16),
            pltpu.VMEM((128, 128), BF16),
            pltpu.VMEM((16, 2, 128, 256), BF16),
            pltpu.VMEM((4, 512, 256), F32),
            pltpu.SemaphoreType.DMA((COUNT,)),
            pltpu.SemaphoreType.DMA((COUNT,)),
        ],
        compiler_params=pltpu.CompilerParams(
            collective_id=0, has_side_effects=True, vmem_limit_bytes=48 << 20
        ),
        name="window",
    )(ints, sources, denom)
    return density.transpose(1, 0, 2)


def solution(mesh):
    in_specs = (P(("aux", "occ"), None, None), P(), P(), P(), P(), P())
    out_specs = P("aux", "occ", None)
    return jax.shard_map(local, mesh=mesh, in_specs=in_specs, out_specs=out_specs, check_vma=False)
```

time: 641 us -> 116 us (0.18)
  waiting for transfers between devices: 543 us -> 0 us
  Pallas kernels: 0 us -> 94.9 us
  starting transfers between devices: 18.3 us -> 0 us
  between operations: 27.5 us -> 9.69 us
  local copies, waits for them, and re-layouts: 26.8 us -> 9.2 us
  other arithmetic: 16.9 us -> 1.3 us
  matrix products: 8.38 us -> 0 us
    psum x2 -> x0, waiting for transfers between devices: 504 us -> none  [the longest x1 300 us: local(): pair_sum = lax.psum(partial_value, 'aux')]
    pallas_call x0 -> x1, Pallas kernels: none -> 94.9 us  [local(): pl.pallas_call(kernel, out_shape=jax.ShapeDtypeStruct((4, 512, 256), BF16...]
    all_to_all x1 -> x0, waiting for transfers between devices: 38.6 us -> none  [local(): lax.all_to_all(integrals, 'occ', split_axis=1, concat_axis=0, tiled=True)]
    all_to_all x1 -> x0, starting transfers between devices: 18.2 us -> none  [local(): lax.all_to_all(integrals, 'occ', split_axis=1, concat_axis=0, tiled=True)]
    convert_element_type x5 -> x0, other arithmetic: 13 us -> none  [the longest x4 6.8 us: local(): (2.0 * scaled_wide - jnp.transpose(scaled_wide, (0, 2, 1))).astype(jnp.bf...]
    convert_element_type x7 -> x0, local copies, waits for them, and re-layouts: 10.3 us -> none  [the longest x3 5.33 us: local(): (2.0 * scaled_wide - jnp.transpose(scaled_wide, (0, 2, 1))).astype(jnp.bf...]
    dot_general x8 -> x0, matrix products: 8.38 us -> none  [the longest x4 5.57 us: local(): lax.dot_general(source, amplitude.reshape(occ_count * virt_count, virt_co...]
  transfers between devices with their start and end apart: 3 -> 0, of which waited for: 3 -> 0; matrix products, arithmetic and copies ran while one was open for 1% -> 0% of each run, Pallas kernels for 0% -> 0%
where the time goes in v1:
time: 116 us; the launch traced here: 115 us
  Pallas kernels  94.9 us (82%)
  between operations  9.69 us (8%)
  local copies, waits for them, and re-layouts  9.2 us (8%)
  other arithmetic  1.3 us (1%)
    pallas_call x1, Pallas kernels, local(): pl.pallas_call(kernel, out_shape=jax.ShapeDtypeStruct((4, 512, 256), BF16...  94.9 us
    reshape x2, local copies, waits for them, and re-layouts, local(): jnp.transpose(integrals, (1, 0, 2)).reshape(4, 4, 4, 32, 2, 128)  2.57 us

profile of v1, /device:TPU:1, one launch (start us, length us, event | category | flops | bytes accessed | tf_op | source)
XLA Modules:
  0.0 115.1 jit_solution(15963919538050158943)
XLA Ops:
  1.3 0.8 dynamic_slice.37
  2.1 0.0 copy-start
  2.1 0.8 dynamic_slice.38
  2.9 0.0 copy-done
  2.9 0.7 fusion.1
  11.9 1.4 %fusion = (f32[1]{0:T(128)}, f32[1]{0:T(128)}) fusion(f32[1024]{0:T(1024)} %param.7, s32[]{:T(128)S(6)} %select_n.81, s32[]{:T(128)S(6)} %select_n.84), kind=kLoop, calls=%fused_computation.11 | loop fusion | bytes 24 | tf_op jit(solution)/shard_map/jit(dynamic_index_in_dim)/dynamic_slice | solution.py:274
  13.2 1.3 %subtract_subtract_fusion.den_ref = f32[128,256]{1,0:T(8,128)S(1)} fusion(f32[]{:T(128)} %bitcast.14, f32[]{:T(128)} %bitcast.12, f32[256]{0:T(256)S(1)} %dynamic_slice.38, f32[128]{0:T(128)S(1)} %dynamic_slice.37), kind=kLoop, calls=%fused_computation.1 | loop fusion | flops 98304 | bytes 132616 | tf_op jit(solution)/shard_map/sub | solution.py:278
  14.5 1.3 %constant_dynamic-slice_fusion.3 = (bf16[32,1,256]{2,1,0:T(2,128)(2,1)S(1)}, bf16[32,1,256]{2,1,0:T(2,128)(2,1)S(1)}, bf16[32,1,256]{2,1,0:T(2,128)(2,1)S(1)}, bf16[32,1,256]{2,1,0:T(2,128)(2,1)S(1)}) fusion(bf16[32,64,256]{2,1,0:T(8,128)(2,1)} %param.6, s32[]{:T(128)S(6)} %select_n.66, s32[]{:T(128)S(6)} %select_n.68, s32[]{:T(128)S(6)} %select_n.67, ...), kind=kLoop, calls=%fused_computation.10 | loop fusion | bytes 131088 | tf_op jit(solution)/shard_map/jit(dynamic_index_in_dim)/dynamic_slice | solution.py:270
  15.8 1.3 %reshape.10 = bf16[4,4,4,32,2,128]{5,4,2,1,0,3:T(2,128)(2,1)S(1)} reshape(bf16[64,32,256]{2,0,1:T(8,128)(2,1)} %bitcast.31) | data formatting | bytes 2097152 | tf_op jit(solution)/shard_map/reshape | solution.py:268
  17.2 1.2 %copy.26 = bf16[4,4,4,32,2,128]{5,3,4,2,1,0:T(8,128)(2,1)S(1)} copy(bf16[4,4,4,32,2,128]{5,4,2,1,0,3:T(2,128)(2,1)S(1)} %reshape.10) | data formatting | bytes 2097152 | tf_op jit(solution)/shard_map/reshape | solution.py:268
  18.4 94.9 %window.1 = bf16[4,512,256]{2,1,0:T(8,128)(2,1)S(1)} custom-call(bf16[4,4,4,2,32,128]{5,4,3,2,1,0:T(8,128)(2,1)S(1)} %bitcast.29, bf16[4,32,256]{2,1,0:T(8,128)(2,1)S(1)} %pad_maximum_fusion.s_ref, f32[128,256]{1,0:T(8,128)S(1)} %subtract_subtract_fusion.den_ref), custom_call_target="tpu_custom_call" | custom-call | tf_op jit(solution)/shard_map/window/pallas_call | solution.py:280
  113.3 1.8 %copy.14 = bf16[512,4,256]{2,1,0:T(4,128)(2,1)} copy(bf16[512,4,256]{2,0,1:T(8,128)(2,1)S(1)} %bitcast.30) | data formatting | bytes 2097152 | tf_op jit(solution)/shard_map/transpose | solution.py:305
  (3 shorter events, 0.0 us)
Async XLA Ops:
  2.1 0.8 copy-start

commit v2 on v0

v2 whole, which is shorter than its diff:
```python
import jax
import jax.numpy as jnp
from jax import lax
from jax.experimental import pallas as pl
from jax.experimental.pallas import tpu as pltpu
from jax.sharding import PartitionSpec as P

MESH = pl.DeviceIdType.MESH
F32, BF16 = jnp.float32, jnp.bfloat16

Q = 4
SIZES = dict(A=96, SRC1=6, SRC2=6, FWD=8, ZG=4, XG=3, RING=16 * Q, AZ=3, AY=12, AR=8, AC=16, LOCAL=3)
SLOT, COUNT = {}, 0
for _name, _size in SIZES.items():
    SLOT[_name] = COUNT
    COUNT += _size
ORDER = (1, 3, 2)
CHUNKS = ((0, 1), (1, 3), (3, 4))


def coords():
    occ, aux = lax.axis_index("occ"), lax.axis_index("aux")
    return occ // 4, (aux // 2) % 4, (occ % 4) * 4 + aux // 8, aux % 2


def device(x, y, z, c):
    return {"occ": x * 4 + z // 4, "aux": ((z % 4) * 4 + y) * 2 + c}


def place(delta):
    low, high = delta % 2, delta // 2
    return 3 - 2 * low - 3 * high + 4 * low * high


def kernel(
    a_ref, eo_ref, ev_ref, so_ref, oo_ref, vo_ref, d_ref,
    arel, own_s, den, ar, at, sr, sd, cc, rb, sb, amp, dacc, snd, rcv,
):
    x, y, z, c = coords()
    zh, zl = z // 4, z % 4
    sends = []

    def copy(src, dst, slot, dev):
        return pltpu.make_async_remote_copy(
            src_ref=src, dst_ref=dst, send_sem=snd.at[slot], recv_sem=rcv.at[slot],
            device_id=dev, device_id_type=MESH,
        )

    def start(cp):
        cp.start()
        sends.append(cp)
        return cp

    barrier = pltpu.get_barrier_semaphore()

    def greet(dev):
        pl.semaphore_signal(barrier, inc=1, device_id=dev, device_id_type=MESH)

    greet(device(x, y, (z + 4) % 16, c))
    greet(device(x, y, (z + 12) % 16, c))

    @pl.loop(1, 32)
    def _(o):
        greet(device((x + o // 8) % 4, (y + (o // 2) % 4) % 4, z, (c + o) % 2))

    greet(device(x, y, (z + 1) % 16, c))
    greet(device(x, y, (z + 15) % 16, c))
    for j in ORDER:
        greet(device(x, y, zh * 4 + (zl + j) % 4, c))

    @pl.loop(0, 4)
    def _(tx):
        rows = a_ref[:, pl.ds(pl.multiple_of(tx * 16, 16), 16), :]
        turned = jnp.swapaxes(rows, 0, 1)
        for h in range(4):
            pos = place((h + 4 - zh) % 4)
            for ty in range(4):
                for tc in range(2):
                    arel[tx, pos, ty, tc] = turned[h * 4 + ty][:, tc * 128:(tc + 1) * 128]

    for s in range(4):
        j = so_ref[s]
        pos = place(((j // 4) % 4 + 4 - zh) % 4)
        for tc in range(2):
            own_s[s, :, tc * 128:(tc + 1) * 128] = arel[j // 16, pos, j % 4, tc]

    first_occ, first_vir = oo_ref[0], vo_ref[0]
    e_occ = eo_ref[first_occ + (x * 4 + zh) * 4 + y]
    e_src = eo_ref[first_occ + so_ref[zl]]
    row, lane = first_vir // 128, first_vir % 128
    window = jnp.concatenate(
        [ev_ref[pl.ds(row, 1), :], ev_ref[pl.ds(row + 1, 1), :], ev_ref[pl.ds(jnp.minimum(row + 2, 31), 1), :]], axis=1
    )

    def column(count, offset):
        at_lane = lax.broadcasted_iota(jnp.int32, (count, 384), 1)
        wanted = lax.broadcasted_iota(jnp.int32, (count, 384), 0) + offset
        return jnp.sum(jnp.where(at_lane == wanted, window, 0.0), axis=1, keepdims=True)

    whole = column(256, lane)
    diagonal = lax.broadcasted_iota(jnp.int32, (256, 256), 0) == lax.broadcasted_iota(jnp.int32, (256, 256), 1)
    vir_b = jnp.sum(jnp.where(diagonal, whole, 0.0), axis=0, keepdims=True)
    den[...] = column(128, lane + c * 128) + vir_b - e_occ - e_src

    pl.semaphore_wait(barrier, 38)

    local = [
        pltpu.make_async_copy(arel.at[x, :, y, c], ar.at[:, x, y, c], rcv.at[SLOT["LOCAL"]]),
        pltpu.make_async_copy(own_s, sr.at[:, x, y, c], rcv.at[SLOT["LOCAL"] + 1]),
        pltpu.make_async_copy(own_s, sd.at[:, x, zh], rcv.at[SLOT["LOCAL"] + 2]),
    ]
    for cp in local:
        cp.start()

    xs = {j: (x + j) % 4 for j in (1, 2, 3)}
    ys = {j: (y + j) % 4 for j in (1, 2, 3)}
    src1 = []
    for j in ORDER:
        src1.append(start(copy(own_s.at[0:2], sr.at[0:2, x, y, c], SLOT["SRC1"] + j - 1, device(xs[j], y, z, c))))
        src1.append(start(copy(own_s.at[2:4], sr.at[2:4, x, y, c], SLOT["SRC1"] + 2 + j, device(x, ys[j], z, c))))
    up4, down4 = device(x, y, (z + 4) % 16, c), device(x, y, (z + 12) % 16, c)
    zg = [
        start(copy(own_s, sd.at[:, x, zh], SLOT["ZG"], up4)),
        start(copy(own_s, sd.at[:, x, zh], SLOT["ZG"] + 1, down4)),
    ]

    def a_copy(o, chunk):
        lo, hi = CHUNKS[chunk]
        tx, ty, tc = (x + o // 8) % 4, (y + (o // 2) % 4) % 4, (c + o) % 2
        return copy(
            arel.at[tx, lo:hi, ty, tc], ar.at[lo:hi, x, y, c], SLOT["A"] + chunk * 32 + o, device(tx, ty, z, tc)
        )

    def a_each(chunk, act):
        @pl.loop(1, 32)
        def _(o):
            act(a_copy(o, chunk))

    a_each(0, lambda cp: cp.start())
    for cp in local:
        cp.wait()
    other = device(x, y, z, 1 - c)
    for cp in src1:
        cp.wait_recv()
    vx, vy = sr.at[0:2, :, y, c], sr.at[2:4, x, :, c]
    src2 = []
    for j in ORDER:
        src2.append(start(copy(vx, vx, SLOT["SRC2"] + j - 1, device(x, ys[j], z, c))))
        src2.append(start(copy(vy, vy, SLOT["SRC2"] + 2 + j, device(xs[j], y, z, c))))
    fwd = [start(copy(v, v, SLOT["FWD"] + n, other)) for n, v in enumerate((vx, vy))]
    a_each(1, lambda cp: cp.start())
    a_each(2, lambda cp: cp.start())
    for n, j in enumerate(ORDER):
        for k, view in enumerate((sr.at[0:2, :, (y + 4 - j) % 4, c], sr.at[2:4, (x + 4 - j) % 4, :, c])):
            src2[2 * n + k].wait_recv()
            fwd.append(start(copy(view, view, SLOT["FWD"] + 2 + 2 * n + k, other)))

    for k, cp in enumerate(list(zg)):
        cp.wait_recv()
        view = sd.at[0:2, x, (zh + 3) % 4] if k == 0 else sd.at[2:4, x, (zh + 1) % 4]
        zg.append(start(copy(view, view, SLOT["ZG"] + 2 + k, (up4, down4)[k])))

    def pairs(chunk, wait=()):
        lo, hi = CHUNKS[chunk]
        a_each(chunk, lambda cp: cp.wait_recv())
        for h in range(lo, hi):
            at[h * 128:(h + 1) * 128, :] = ar[h].reshape(1024, 128).T
        for cp in wait:
            cp.wait_recv()

        @pl.loop(0, 4)
        def _(s):
            part = jnp.dot(at[lo * 128:hi * 128, :], sr[s].reshape(1024, 256), preferred_element_type=F32)
            for h in range(lo, hi):
                cc[h * 4 + s] = part[(h - lo) * 128:(h - lo + 1) * 128]

    up, down = device(x, y, (z + 1) % 16, c), device(x, y, (z + 15) % 16, c)
    span = 128 // Q

    def hop(way, d, q):
        slot = SLOT["RING"] + (way * 8 + d - 1) * Q + q
        return copy(sb.at[way, d - 1, q], rb.at[way, d - 1, q], slot, up if way == 0 else down)

    def send(way, d, q, add):
        ahead = d if way == 0 else 16 - d
        target = (z + ahead) % 16
        spot = place((target // 4 + 4 - zh) % 4) * 4 + target % 4
        value = cc[spot, pl.ds(q * span, span), :]
        if add:
            hop(way, d + 1, q).wait_recv()
            value = value + rb[way, d, q].astype(F32)
        sb[way, d - 1, q] = value.astype(BF16)
        hop(way, d, q).start()

    def steps(lo, hi):
        @pl.loop(lo, hi)
        def _(k):
            for q in range(Q):
                send(0, 8 - k, q, True)
                send(1, 7 - k, q, True)

    def flush():
        for chunk in range(3):
            a_each(chunk, lambda cp: cp.wait_send())
        for cp in sends:
            cp.wait_send()

    def flush_ring():
        for q in range(Q):
            hop(0, 8, q).wait_send()

            @pl.loop(1, 8)
            def _(d, q=q):
                hop(0, d, q).wait_send()
                hop(1, d, q).wait_send()

    pairs(0, fwd)
    for q in range(Q):
        send(0, 8, q, False)
    pairs(1)
    for q in range(Q):
        send(1, 7, q, False)
    steps(1, 4)
    pairs(2)
    for cp in zg[2:]:
        cp.wait_recv()
    vd = sd.at[:, x]
    xg = [start(copy(vd, vd, SLOT["XG"] + j - 1, device(xs[j], y, z, c))) for j in ORDER]
    steps(4, 7)
    for q in range(Q):
        send(0, 1, q, True)

    own = amp.at[y * 4 + zl, c]
    mine = place(0) * 4 + zl
    for q in range(Q):
        rows = pl.ds(q * span, span)
        hop(1, 1, q).wait_recv()
        total = cc[mine, rows, :] + rb[1, 0, q].astype(F32)
        hop(0, 1, q).wait_recv()
        total = total + rb[0, 0, q].astype(F32)
        own[rows, :] = (total / den[rows, :]).astype(BF16)

    def block(j, m):
        return (y + 4 - m) % 4 * 4 + (zl + 4 - j) % 4

    def to_z(j):
        return copy(own, own, SLOT["AZ"] + j - 1, device(x, y, zh * 4 + (zl + j) % 4, c))

    def to_y(j, m):
        view = amp.at[block(j, 0), c]
        return copy(view, view, SLOT["AY"] + j * 3 + m - 1, device(x, ys[m], z, c))

    def relay(j, half):
        view = amp.at[block(j, (1, 3)[half]), c, half * 64:(half + 1) * 64]
        return copy(view, view, SLOT["AR"] + j * 2 + half, device(x, ys[(1, 3)[half]], z, c))

    def to_core(j, m):
        view = amp.at[block(j, m), c]
        return copy(view, view, SLOT["AC"] + j * 4 + m, other)

    touched = set()

    def product(j, m, last=False):
        to_core(j, m).wait_recv()
        b = block(j, m)
        t, s = b // 4, b % 4
        lhs, rhs = sd[s].reshape(512, 256), amp[b].reshape(256, 256)
        straight = lax.dot_general(lhs, rhs, (((1,), (1,)), ((), ())), preferred_element_type=F32)
        crossed = jnp.dot(lhs, rhs, preferred_element_type=F32)
        value = 2.0 * straight - crossed
        if m in touched:
            value = dacc[t] + value
        touched.add(m)
        if last:
            d_ref[t] = value.astype(BF16)
        else:
            dacc[t] = value

    turn = (0, 1, 3, 2)
    for j in turn:
        if j:
            to_z(j).wait_recv()
        start(to_y(j, 1))
        start(to_y(j, 3))
        if not j:
            for k in ORDER:
                start(to_z(k))
        start(to_core(j, 0))
    for cp in xg:
        cp.wait_recv()
    for n, j in enumerate(turn):
        for half, m in enumerate((1, 3)):
            to_y(j, m).wait_recv()
            start(relay(j, half))
            start(to_core(j, m))
        if n:
            for m in (0, 1, 3):
                product(turn[n - 1], m)
    for n, j in enumerate(turn):
        for half in range(2):
            relay(j, half).wait_recv()
        start(to_core(j, 2))
        if n == 0:
            for m in (0, 1, 3):
                product(turn[3], m, True)
        else:
            product(turn[n - 1], 2)
    product(turn[3], 2, True)
    flush()
    flush_ring()


def window(integrals, eps_occ, eps_vir, src_occ, occ_offset, vir_offset):
    vmem, smem = pl.BlockSpec(memory_space=pltpu.VMEM), pl.BlockSpec(memory_space=pltpu.SMEM)
    return pl.pallas_call(
        kernel,
        out_shape=jax.ShapeDtypeStruct((4, 512, 256), BF16),
        in_specs=[vmem, smem, vmem, smem, smem, smem],
        out_specs=vmem,
        scratch_shapes=[
            pltpu.VMEM((4, 4, 4, 2, 32, 128), BF16),
            pltpu.VMEM((4, 32, 256), BF16),
            pltpu.VMEM((128, 256), F32),
            pltpu.VMEM((4, 4, 4, 2, 32, 128), BF16),
            pltpu.VMEM((512, 1024), BF16),
            pltpu.VMEM((4, 4, 4, 2, 32, 256), BF16),
            pltpu.VMEM((4, 4, 4, 32, 256), BF16),
            pltpu.VMEM((16, 128, 256), F32),
            pltpu.VMEM((2, 8, Q, 128 // Q, 256), BF16),
            pltpu.VMEM((2, 8, Q, 128 // Q, 256), BF16),
            pltpu.VMEM((16, 2, 128, 256), BF16),
            pltpu.VMEM((4, 512, 256), F32),
            pltpu.SemaphoreType.DMA((COUNT,)),
            pltpu.SemaphoreType.DMA((COUNT,)),
        ],
        compiler_params=pltpu.CompilerParams(
            collective_id=0, has_side_effects=True, vmem_limit_bytes=48 << 20
        ),
        name="window",
    )(integrals, eps_occ, eps_vir.reshape(32, 128), src_occ, occ_offset, vir_offset)


def local(*args):
    return window(*args).transpose(1, 0, 2)


def solution(mesh):
    in_specs = (P(("aux", "occ"), None, None), P(), P(), P(), P(), P())
    out_specs = P("aux", "occ", None)
    return jax.shard_map(local, mesh=mesh, in_specs=in_specs, out_specs=out_specs, check_vma=False)
```

time: 641 us -> 88.8 us (0.14)
  waiting for transfers between devices: 543 us -> 0 us
  Pallas kernels: 0 us -> 82.9 us
  between operations: 27.5 us -> 1.34 us
  local copies, waits for them, and re-layouts: 26.8 us -> 4.36 us
  starting transfers between devices: 18.3 us -> 0 us
  other arithmetic: 16.9 us -> 0 us
  matrix products: 8.38 us -> 0 us
    psum x2 -> x0, waiting for transfers between devices: 504 us -> none  [the longest x1 300 us: local(): pair_sum = lax.psum(partial_value, 'aux')]
    pallas_call x0 -> x1, Pallas kernels: none -> 82.9 us  [window(): pl.pallas_call(kernel, out_shape=jax.ShapeDtypeStruct((4, 512, 256), BF16...]
    all_to_all x1 -> x0, waiting for transfers between devices: 38.6 us -> none  [local(): lax.all_to_all(integrals, 'occ', split_axis=1, concat_axis=0, tiled=True)]
    all_to_all x1 -> x0, starting transfers between devices: 18.2 us -> none  [local(): lax.all_to_all(integrals, 'occ', split_axis=1, concat_axis=0, tiled=True)]
    convert_element_type x5 -> x0, other arithmetic: 13 us -> none  [the longest x4 6.8 us: local(): (2.0 * scaled_wide - jnp.transpose(scaled_wide, (0, 2, 1))).astype(jnp.bf...]
    convert_element_type x7 -> x0, local copies, waits for them, and re-layouts: 10.3 us -> none  [the longest x3 5.33 us: local(): (2.0 * scaled_wide - jnp.transpose(scaled_wide, (0, 2, 1))).astype(jnp.bf...]
    dot_general x8 -> x0, matrix products: 8.38 us -> none  [the longest x4 5.57 us: local(): lax.dot_general(source, amplitude.reshape(occ_count * virt_count, virt_co...]
    reshape x5 -> x0, local copies, waits for them, and re-layouts: 6.87 us -> none  [the longest x4 5.29 us: local(): partial_value = partial_value.reshape(occ_count, virt_count, virt_count)]
  transfers between devices with their start and end apart: 3 -> 0, of which waited for: 3 -> 0; matrix products, arithmetic and copies ran while one was open for 1% -> 0% of each run, Pallas kernels for 0% -> 0%
where the time goes in v2:
time: 88.8 us; the launch traced here: 88.6 us
  Pallas kernels  82.9 us (93%)
  local copies, waits for them, and re-layouts  4.36 us (5%)
  between operations  1.34 us (2%)
    pallas_call x1, Pallas kernels, window(): pl.pallas_call(kernel, out_shape=jax.ShapeDtypeStruct((4, 512, 256), BF16...  82.9 us
    unnamed x8, local copies, waits for them, and re-layouts  2.58 us
    transpose x1, local copies, waits for them, and re-layouts, local(): return window(*args).transpose(1, 0, 2)  1.78 us

profile of v2, /device:TPU:1, one launch (start us, length us, event | category | flops | bytes accessed | tf_op | source)
XLA Modules:
  0.0 88.6 jit_solution(5136620674827527842)
XLA Ops:
  0.0 0.0 copy-start.2
  1.3 0.0 copy-start.3
  1.3 0.0 copy-done.2
  1.3 0.6 copy-done.3
  2.0 0.0 copy-start
  2.0 1.2 %copy-done = bf16[32,64,256]{2,1,0:T(8,128)(2,1)S(1)} copy-done((bf16[32,64,256]{2,1,0:T(8,128)(2,1)S(1)}, bf16[32,64,256]{2,1,0:T(8,128)(2,1)}, u32[]{:S(2)}) %copy-start) | copy-done | bytes 1048600
  3.2 0.0 copy-start.1
  3.2 0.7 copy-done.1
  3.9 82.9 %window.1 = bf16[4,512,256]{2,1,0:T(8,128)(2,1)S(1)} custom-call(bf16[32,64,256]{2,1,0:T(8,128)(2,1)S(1)} %copy-done, f32[1024]{0:T(1024)S(1)} %copy-done.2, f32[32,128]{1,0:T(8,128)S(1)} %bitcast.3, s32[4]{0:T(128)S(1)} %copy-done.3, s32[1]{0:T(128)S(6)} %copy.8.oo_ref, s32[1]{0:T(128)S(6)} %copy.9.vo_ref), custom_call_target="tpu_custom_call" | custom-call | tf_op jit(solution)/shard_map/window/pallas_call | solution.py:315
  86.8 1.8 %copy.7 = bf16[512,4,256]{2,1,0:T(4,128)(2,1)} copy(bf16[512,4,256]{2,0,1:T(8,128)(2,1)S(1)} %bitcast.2) | data formatting | bytes 2097152 | tf_op jit(solution)/shard_map/transpose | solution.py:344
Async XLA Ops:
  0.0 1.3 %copy-start.2 = (f32[1024]{0:T(1024)S(1)}, f32[1024]{0:T(1024)}, u32[]{:S(2)}) copy-start(f32[1024]{0:T(1024)} %eo_ref.1) | copy-start | bytes 12292
  1.3 0.7 copy-start.3
  2.0 1.2 %copy-start = (bf16[32,64,256]{2,1,0:T(8,128)(2,1)S(1)}, bf16[32,64,256]{2,1,0:T(8,128)(2,1)}, u32[]{:S(2)}) copy-start(bf16[32,64,256]{2,1,0:T(8,128)(2,1)} %a_ref.1) | copy-start | bytes 3145732
  3.2 0.7 copy-start.1

commit v3 on v2

--- a/solution.py
+++ b/solution.py
@@ -9,13 +9,13 @@
 F32, BF16 = jnp.float32, jnp.bfloat16
 
 Q = 4
-SIZES = dict(A=96, SRC1=6, SRC2=6, FWD=8, ZG=4, XG=3, RING=16 * Q, AZ=3, AY=12, AR=8, AC=16, LOCAL=3)
+SIZES = dict(A=128, SRC1=6, SRC2=6, FWD=8, ZG=4, XG=3, RING=16 * Q, AZ=6, AY=24, AR=8, AC=32, LOCAL=3, LOAD=6)
 SLOT, COUNT = {}, 0
 for _name, _size in SIZES.items():
     SLOT[_name] = COUNT
     COUNT += _size
 ORDER = (1, 3, 2)
-CHUNKS = ((0, 1), (1, 3), (3, 4))
+CHUNKS = ((0, 1), (1, 2), (2, 3), (3, 4))
 
 
 def coords():
@@ -33,7 +33,8 @@
 
 
 def kernel(
-    a_ref, eo_ref, ev_ref, so_ref, oo_ref, vo_ref, d_ref,
+    a_hbm, eo_hbm, ev_hbm, so_hbm, oo_hbm, vo_hbm, d_ref,
+    a_ref, eo_ref, ev_ref, so_ref, oo_ref, vo_ref,
     arel, own_s, den, ar, at, sr, sd, cc, rb, sb, amp, dacc, snd, rcv,
 ):
     x, y, z, c = coords()
@@ -51,6 +52,14 @@
         sends.append(cp)
         return cp
 
+    loads = [
+        pltpu.make_async_copy(src, dst, rcv.at[SLOT["LOAD"] + n])
+        for n, (src, dst) in enumerate((
+            (so_hbm, so_ref), (a_hbm, a_ref), (oo_hbm, oo_ref), (vo_hbm, vo_ref), (eo_hbm, eo_ref), (ev_hbm, ev_ref),
+        ))
+    ]
+    for cp in loads:
+        cp.start()
     barrier = pltpu.get_barrier_semaphore()
 
     def greet(dev):
@@ -68,44 +77,25 @@
     for j in ORDER:
         greet(device(x, y, zh * 4 + (zl + j) % 4, c))
 
-    @pl.loop(0, 4)
-    def _(tx):
-        rows = a_ref[:, pl.ds(pl.multiple_of(tx * 16, 16), 16), :]
-        turned = jnp.swapaxes(rows, 0, 1)
-        for h in range(4):
-            pos = place((h + 4 - zh) % 4)
-            for ty in range(4):
-                for tc in range(2):
-                    arel[tx, pos, ty, tc] = turned[h * 4 + ty][:, tc * 128:(tc + 1) * 128]
-
-    for s in range(4):
-        j = so_ref[s]
-        pos = place(((j // 4) % 4 + 4 - zh) % 4)
-        for tc in range(2):
-            own_s[s, :, tc * 128:(tc + 1) * 128] = arel[j // 16, pos, j % 4, tc]
-
-    first_occ, first_vir = oo_ref[0], vo_ref[0]
-    e_occ = eo_ref[first_occ + (x * 4 + zh) * 4 + y]
-    e_src = eo_ref[first_occ + so_ref[zl]]
-    row, lane = first_vir // 128, first_vir % 128
-    window = jnp.concatenate(
-        [ev_ref[pl.ds(row, 1), :], ev_ref[pl.ds(row + 1, 1), :], ev_ref[pl.ds(jnp.minimum(row + 2, 31), 1), :]], axis=1
-    )
-
-    def column(count, offset):
-        at_lane = lax.broadcasted_iota(jnp.int32, (count, 384), 1)
-        wanted = lax.broadcasted_iota(jnp.int32, (count, 384), 0) + offset
-        return jnp.sum(jnp.where(at_lane == wanted, window, 0.0), axis=1, keepdims=True)
-
-    whole = column(256, lane)
-    diagonal = lax.broadcasted_iota(jnp.int32, (256, 256), 0) == lax.broadcasted_iota(jnp.int32, (256, 256), 1)
-    vir_b = jnp.sum(jnp.where(diagonal, whole, 0.0), axis=0, keepdims=True)
-    den[...] = column(128, lane + c * 128) + vir_b - e_occ - e_src
+    for cp in loads:
+        cp.wait()
+    row16 = lax.broadcasted_iota(jnp.int32, (16, 16, 256), 1)
+
+    @pl.loop(0, 2)
+    def _(p):
+        lines = pl.ds(pl.multiple_of(p * 16, 16), 16)
+        found = [jnp.zeros((16, 256), F32)] * 4
+        for g in range(4):
+            rows = a_ref[lines, g * 16:(g + 1) * 16, :].astype(F32)
+            found = [
+                found[s] + jnp.sum(jnp.where(row16 == so_ref[s] - g * 16, rows, 0.0), axis=1) for s in range(4)
+            ]
+        for s in range(4):
+            own_s[s, lines, :] = found[s].astype(BF16)
 
     pl.semaphore_wait(barrier, 38)
 
     local = [
-        pltpu.make_async_copy(arel.at[x, :, y, c], ar.at[:, x, y, c], rcv.at[SLOT["LOCAL"]]),
         pltpu.make_async_copy(own_s, sr.at[:, x, y, c], rcv.at[SLOT["LOCAL"] + 1]),
         pltpu.make_async_copy(own_s, sd.at[:, x, zh], rcv.at[SLOT["LOCAL"] + 2]),
     ]
@@ -136,7 +126,18 @@
         def _(o):
             act(a_copy(o, chunk))
 
-    a_each(0, lambda cp: cp.start())
+    @pl.loop(0, 4)
+    def _(tx):
+        rows = a_ref[:, pl.ds(pl.multiple_of(tx * 16, 16), 16), :]
+        turned = jnp.swapaxes(rows, 0, 1)
+        for h in range(4):
+            pos = place((h + 4 - zh) % 4)
+            for ty in range(4):
+                for tc in range(2):
+                    arel[tx, pos, ty, tc] = turned[h * 4 + ty][:, tc * 128:(tc + 1) * 128]
+
+    keep = pltpu.make_async_copy(arel.at[x, :, y, c], ar.at[:, x, y, c], rcv.at[SLOT["LOCAL"]])
+    keep.start()
     for cp in local:
         cp.wait()
     other = device(x, y, z, 1 - c)
@@ -148,8 +149,34 @@
         src2.append(start(copy(vx, vx, SLOT["SRC2"] + j - 1, device(x, ys[j], z, c))))
         src2.append(start(copy(vy, vy, SLOT["SRC2"] + 2 + j, device(xs[j], y, z, c))))
     fwd = [start(copy(v, v, SLOT["FWD"] + n, other)) for n, v in enumerate((vx, vy))]
-    a_each(1, lambda cp: cp.start())
-    a_each(2, lambda cp: cp.start())
+    for chunk in range(4):
+        a_each(chunk, lambda cp: cp.start())
+    first_occ, first_vir = oo_ref[0], vo_ref[0]
+    at_occ = lax.broadcasted_iota(jnp.int32, (8, 128), 0) * 128 + lax.broadcasted_iota(jnp.int32, (8, 128), 1)
+
+    def occupied(index):
+        kept = jnp.where(at_occ == first_occ + index, eo_ref[...], 0.0)
+        return jnp.sum(jnp.sum(kept, axis=1, keepdims=True), axis=0, keepdims=True)
+
+    e_occ = occupied((x * 4 + zh) * 4 + y)
+    e_src = occupied(so_ref[zl])
+    row, lane = first_vir // 128, first_vir % 128
+    at_row = lax.broadcasted_iota(jnp.int32, (32, 128), 0)
+    window = jnp.concatenate(
+        [jnp.sum(jnp.where(at_row == row + n, ev_ref[...], 0.0), axis=0, keepdims=True) for n in range(3)], axis=1
+    )
+
+    def column(count, offset):
+        at_lane = lax.broadcasted_iota(jnp.int32, (count, 384), 1)
+        wanted = lax.broadcasted_iota(jnp.int32, (count, 384), 0) + offset
+        return jnp.sum(jnp.where(at_lane == wanted, window, 0.0), axis=1, keepdims=True)
+
+    whole = column(256, lane)
+    diagonal = lax.broadcasted_iota(jnp.int32, (256, 256), 0) == lax.broadcasted_iota(jnp.int32, (256, 256), 1)
+    vir_b = jnp.sum(jnp.where(diagonal, whole, 0.0), axis=0, keepdims=True)
+    den[...] = column(128, lane + c * 128) + vir_b - e_occ - e_src
+
+    keep.wait()
     for n, j in enumerate(ORDER):
         for k, view in enumerate((sr.at[0:2, :, (y + 4 - j) % 4, c], sr.at[2:4, (x + 4 - j) % 4, :, c])):
             src2[2 * n + k].wait_recv()
@@ -160,14 +187,11 @@
         view = sd.at[0:2, x, (zh + 3) % 4] if k == 0 else sd.at[2:4, x, (zh + 1) % 4]
         zg.append(start(copy(view, view, SLOT["ZG"] + 2 + k, (up4, down4)[k])))
 
-    def pairs(chunk, wait=()):
-        lo, hi = CHUNKS[chunk]
+    def turn_over(chunk):
         a_each(chunk, lambda cp: cp.wait_recv())
-        for h in range(lo, hi):
-            at[h * 128:(h + 1) * 128, :] = ar[h].reshape(1024, 128).T
-        for cp in wait:
-            cp.wait_recv()
-
+        at[chunk * 128:(chunk + 1) * 128, :] = ar[chunk].reshape(1024, 128).T
+
+    def pairs(lo, hi):
         @pl.loop(0, 4)
         def _(s):
             part = jnp.dot(at[lo * 128:hi * 128, :], sr[s].reshape(1024, 256), preferred_element_type=F32)
@@ -200,7 +224,7 @@
                 send(1, 7 - k, q, True)
 
     def flush():
-        for chunk in range(3):
+        for chunk in range(4):
             a_each(chunk, lambda cp: cp.wait_send())
         for cp in sends:
             cp.wait_send()
@@ -214,14 +238,20 @@
                 hop(0, d, q).wait_send()
                 hop(1, d, q).wait_send()
 
-    pairs(0, fwd)
+    turn_over(0)
+    for cp in fwd:
+        cp.wait_recv()
+    pairs(0, 1)
     for q in range(Q):
         send(0, 8, q, False)
-    pairs(1)
+    turn_over(1)
+    turn_over(2)
+    pairs(1, 3)
     for q in range(Q):
         send(1, 7, q, False)
     steps(1, 4)
-    pairs(2)
+    turn_over(3)
+    pairs(3, 4)
     for cp in zg[2:]:
         cp.wait_recv()
     vd = sd.at[:, x]
@@ -230,38 +260,51 @@
     for q in range(Q):
         send(0, 1, q, True)
 
-    own = amp.at[y * 4 + zl, c]
     mine = place(0) * 4 + zl
+    part = (pl.ds(0, 64), pl.ds(64, 64))
+
+    def block(j, m):
+        return (y + 4 - m) % 4 * 4 + (zl + 4 - j) % 4
+
+    def to_z(j, h):
+        view = amp.at[block(0, 0), c, part[h]]
+        return copy(view, view, SLOT["AZ"] + (j - 1) * 2 + h, device(x, y, zh * 4 + (zl + j) % 4, c))
+
+    def to_y(j, m, h):
+        view = amp.at[block(j, 0), c, part[h]]
+        return copy(view, view, SLOT["AY"] + (j * 3 + m - 1) * 2 + h, device(x, ys[m], z, c))
+
+    def relay(j, h):
+        view = amp.at[block(j, (1, 3)[h]), c, part[h]]
+        return copy(view, view, SLOT["AR"] + j * 2 + h, device(x, ys[(1, 3)[h]], z, c))
+
+    def to_core(j, m, h):
+        view = amp.at[block(j, m), c, part[h]]
+        return copy(view, view, SLOT["AC"] + (j * 4 + m) * 2 + h, other)
+
+    def spread(j, h):
+        if j == 0:
+            for k in (2, 1, 3):
+                start(to_z(k, h))
+        start(to_y(j, 1, h))
+        start(to_y(j, 3, h))
+        start(to_core(j, 0, h))
+
     for q in range(Q):
         rows = pl.ds(q * span, span)
         hop(1, 1, q).wait_recv()
         total = cc[mine, rows, :] + rb[1, 0, q].astype(F32)
         hop(0, 1, q).wait_recv()
         total = total + rb[0, 0, q].astype(F32)
-        own[rows, :] = (total / den[rows, :]).astype(BF16)
-
-    def block(j, m):
-        return (y + 4 - m) % 4 * 4 + (zl + 4 - j) % 4
-
-    def to_z(j):
-        return copy(own, own, SLOT["AZ"] + j - 1, device(x, y, zh * 4 + (zl + j) % 4, c))
-
-    def to_y(j, m):
-        view = amp.at[block(j, 0), c]
-        return copy(view, view, SLOT["AY"] + j * 3 + m - 1, device(x, ys[m], z, c))
-
-    def relay(j, half):
-        view = amp.at[block(j, (1, 3)[half]), c, half * 64:(half + 1) * 64]
-        return copy(view, view, SLOT["AR"] + j * 2 + half, device(x, ys[(1, 3)[half]], z, c))
-
-    def to_core(j, m):
-        view = amp.at[block(j, m), c]
-        return copy(view, view, SLOT["AC"] + j * 4 + m, other)
+        amp[block(0, 0), c, rows, :] = (total / den[rows, :]).astype(BF16)
+        if (q + 1) * span % 64 == 0:
+            spread(0, (q + 1) * span // 64 - 1)
 
     touched = set()
 
     def product(j, m, last=False):
-        to_core(j, m).wait_recv()
+        for h in range(2):
+            to_core(j, m, h).wait_recv()
         b = block(j, m)
         t, s = b // 4, b % 4
         lhs, rhs = sd[s].reshape(512, 256), amp[b].reshape(256, 256)
@@ -277,47 +320,55 @@
             dacc[t] = value
 
     turn = (0, 1, 3, 2)
+
+    def pass_on(j):
+        for h in range(2):
+            for m in (1, 3):
+                to_y(j, m, h).wait_recv()
+                if m == (1, 3)[h]:
+                    start(relay(j, h))
+                start(to_core(j, m, h))
+
+    for j in turn[1:]:
+        for h in range(2):
+            to_z(j, h).wait_recv()
+            spread(j, h)
     for j in turn:
-        if j:
-            to_z(j).wait_recv()
-        start(to_y(j, 1))
-        start(to_y(j, 3))
-        if not j:
-            for k in ORDER:
-                start(to_z(k))
-        start(to_core(j, 0))
+        pass_on(j)
     for cp in xg:
         cp.wait_recv()
-    for n, j in enumerate(turn):
-        for half, m in enumerate((1, 3)):
-            to_y(j, m).wait_recv()
-            start(relay(j, half))
-            start(to_core(j, m))
-        if n:
-            for m in (0, 1, 3):
-                product(turn[n - 1], m)
-    for n, j in enumerate(turn):
-        for half in range(2):
-            relay(j, half).wait_recv()
-        start(to_core(j, 2))
-        if n == 0:
-            for m in (0, 1, 3):
-                product(turn[3], m, True)
-        else:
-            product(turn[n - 1], 2)
-    product(turn[3], 2, True)
+    for j in turn[:3]:
+        for m in (0, 1, 3):
+            product(j, m)
+
+    def take(j):
+        for h in range(2):
+            relay(j, h).wait_recv()
+            start(to_core(j, 2, h))
+
+    for j in turn:
+        take(j)
+    for m in (0, 1, 3):
+        product(turn[3], m, True)
+    for j in turn:
+        product(j, 2, j == turn[3])
     flush()
     flush_ring()
 
 
 def window(integrals, eps_occ, eps_vir, src_occ, occ_offset, vir_offset):
-    vmem, smem = pl.BlockSpec(memory_space=pltpu.VMEM), pl.BlockSpec(memory_space=pltpu.SMEM)
     return pl.pallas_call(
         kernel,
         out_shape=jax.ShapeDtypeStruct((4, 512, 256), BF16),
-        in_specs=[vmem, smem, vmem, smem, smem, smem],
-        out_specs=vmem,
+        in_specs=[pl.BlockSpec(memory_space=pl.ANY)] * 6,
+        out_specs=pl.BlockSpec(memory_space=pltpu.VMEM),
         scratch_shapes=[
+            pltpu.VMEM((32, 64, 256), BF16),
+            pltpu.VMEM((8, 128), F32),
+            pltpu.VMEM((32, 128), F32),
+            pltpu.SMEM((4,), jnp.int32),
+            pltpu.SMEM((1,), jnp.int32),
+            pltpu.SMEM((1,), jnp.int32),
             pltpu.VMEM((4, 4, 4, 2, 32, 128), BF16),
             pltpu.VMEM((4, 32, 256), BF16),
             pltpu.VMEM((128, 256), F32),
@@ -334,10 +385,10 @@
             pltpu.SemaphoreType.DMA((COUNT,)),
         ],
         compiler_params=pltpu.CompilerParams(
-            collective_id=0, has_side_effects=True, vmem_limit_bytes=48 << 20
+            collective_id=0, has_side_effects=True, vmem_limit_bytes=66 * 10**6
         ),
         name="window",
-    )(integrals, eps_occ, eps_vir.reshape(32, 128), src_occ, occ_offset, vir_offset)
+    )(integrals, eps_occ.reshape(8, 128), eps_vir.reshape(32, 128), src_occ, occ_offset, vir_offset)
 
 
 def local(*args):

time: 88.8 us -> 91.7 us (1.033)
  Pallas kernels: 82.9 us -> 87.2 us
  local copies, waits for them, and re-layouts: 4.36 us -> 3.01 us
    pallas_call x1, Pallas kernels: 82.9 us -> 87.2 us  [window(): pl.pallas_call(kernel, out_shape=jax.ShapeDtypeStruct((4, 512, 256), BF16...]
    unnamed x8 -> x0, local copies, waits for them, and re-layouts: 2.58 us -> none
    transpose x1, local copies, waits for them, and re-layouts: 1.78 us -> 3.01 us  [local(): return window(*args).transpose(1, 0, 2)]
where the time goes in v3:
time: 91.7 us; the launch traced here: 91.5 us
  Pallas kernels  87.2 us (95%)
  local copies, waits for them, and re-layouts  3.01 us (3%)
  between operations  1.3 us (1%)
    pallas_call x1, Pallas kernels, window(): pl.pallas_call(kernel, out_shape=jax.ShapeDtypeStruct((4, 512, 256), BF16...  87.2 us
    transpose x1, local copies, waits for them, and re-layouts, local(): return window(*args).transpose(1, 0, 2)  3.01 us

profile of v3, /device:TPU:1, one launch (start us, length us, event | category | flops | bytes accessed | tf_op | source)
XLA Modules:
  0.0 91.5 jit_solution(10144760264106838180)
XLA Ops:
  1.3 87.2 %window.1 = bf16[4,512,256]{2,1,0:T(8,128)(2,1)} custom-call(bf16[32,64,256]{2,1,0:T(8,128)(2,1)} %a_hbm.1, f32[8,128]{1,0:T(8,128)} %bitcast.5, f32[32,128]{1,0:T(8,128)} %bitcast.4, s32[4]{0:T(128)} %so_hbm.1, s32[1]{0:T(128)S(6)} %copy.8.oo_hbm, s32[1]{0:T(128)S(6)} %copy.9.vo_hbm), custom_call_target="tpu_custom_call" | custom-call | tf_op jit(solution)/shard_map/window/pallas_call | solution.py:360
  88.5 3.0 %copy.7 = bf16[512,4,256]{2,1,0:T(4,128)(2,1)} copy(bf16[512,4,256]{2,0,1:T(8,128)(2,1)} %bitcast.3) | data formatting | bytes 2097152 | tf_op jit(solution)/shard_map/transpose | solution.py:395

commit v4 on v3

--- a/solution.py
+++ b/solution.py
@@ -15,7 +15,7 @@
     SLOT[_name] = COUNT
     COUNT += _size
 ORDER = (1, 3, 2)
-CHUNKS = ((0, 1), (1, 2), (2, 3), (3, 4))
+CHUNKS = ((0, 1), (1, 3), (3, 4))
 
 
 def coords():
@@ -33,8 +33,7 @@
 
 
 def kernel(
-    a_hbm, eo_hbm, ev_hbm, so_hbm, oo_hbm, vo_hbm, d_ref,
-    a_ref, eo_ref, ev_ref, so_ref, oo_ref, vo_ref,
+    a_hbm, eo_hbm, ev_hbm, so_ref, oo_ref, vo_ref, d_ref, a_ref, eo_ref, ev_ref,
     arel, own_s, den, ar, at, sr, sd, cc, rb, sb, amp, dacc, snd, rcv,
 ):
     x, y, z, c = coords()
@@ -55,7 +54,7 @@
     loads = [
         pltpu.make_async_copy(src, dst, rcv.at[SLOT["LOAD"] + n])
         for n, (src, dst) in enumerate((
-            (so_hbm, so_ref), (a_hbm, a_ref), (oo_hbm, oo_ref), (vo_hbm, vo_ref), (eo_hbm, eo_ref), (ev_hbm, ev_ref),
+            (a_hbm, a_ref), (eo_hbm, eo_ref), (ev_hbm, ev_ref),
         ))
     ]
     for cp in loads:
@@ -77,21 +76,23 @@
     for j in ORDER:
         greet(device(x, y, zh * 4 + (zl + j) % 4, c))
 
-    for cp in loads:
+    for cp in loads[:1]:
         cp.wait()
-    row16 = lax.broadcasted_iota(jnp.int32, (16, 16, 256), 1)
-
-    @pl.loop(0, 2)
-    def _(p):
-        lines = pl.ds(pl.multiple_of(p * 16, 16), 16)
-        found = [jnp.zeros((16, 256), F32)] * 4
-        for g in range(4):
-            rows = a_ref[lines, g * 16:(g + 1) * 16, :].astype(F32)
-            found = [
-                found[s] + jnp.sum(jnp.where(row16 == so_ref[s] - g * 16, rows, 0.0), axis=1) for s in range(4)
-            ]
-        for s in range(4):
-            own_s[s, lines, :] = found[s].astype(BF16)
+    @pl.loop(0, 4)
+    def _(tx):
+        rows = a_ref[:, pl.ds(pl.multiple_of(tx * 16, 16), 16), :]
+        turned = jnp.swapaxes(rows, 0, 1)
+        for h in range(4):
+            pos = place((h + 4 - zh) % 4)
+            for ty in range(4):
+                for tc in range(2):
+                    arel[tx, pos, ty, tc] = turned[h * 4 + ty][:, tc * 128:(tc + 1) * 128]
+
+    for s in range(4):
+        j = so_ref[s]
+        pos = place(((j // 4) % 4 + 4 - zh) % 4)
+        for tc in range(2):
+            own_s[s, :, tc * 128:(tc + 1) * 128] = arel[j // 16, pos, j % 4, tc]
 
     pl.semaphore_wait(barrier, 38)
 
@@ -126,16 +127,6 @@
         def _(o):
             act(a_copy(o, chunk))
 
-    @pl.loop(0, 4)
-    def _(tx):
-        rows = a_ref[:, pl.ds(pl.multiple_of(tx * 16, 16), 16), :]
-        turned = jnp.swapaxes(rows, 0, 1)
-        for h in range(4):
-            pos = place((h + 4 - zh) % 4)
-            for ty in range(4):
-                for tc in range(2):
-                    arel[tx, pos, ty, tc] = turned[h * 4 + ty][:, tc * 128:(tc + 1) * 128]
-
     keep = pltpu.make_async_copy(arel.at[x, :, y, c], ar.at[:, x, y, c], rcv.at[SLOT["LOCAL"]])
     keep.start()
     for cp in local:
@@ -149,8 +140,10 @@
         src2.append(start(copy(vx, vx, SLOT["SRC2"] + j - 1, device(x, ys[j], z, c))))
         src2.append(start(copy(vy, vy, SLOT["SRC2"] + 2 + j, device(xs[j], y, z, c))))
     fwd = [start(copy(v, v, SLOT["FWD"] + n, other)) for n, v in enumerate((vx, vy))]
-    for chunk in range(4):
+    for chunk in range(3):
         a_each(chunk, lambda cp: cp.start())
+    for cp in loads[1:]:
+        cp.wait()
     first_occ, first_vir = oo_ref[0], vo_ref[0]
     at_occ = lax.broadcasted_iota(jnp.int32, (8, 128), 0) * 128 + lax.broadcasted_iota(jnp.int32, (8, 128), 1)
 
@@ -189,7 +182,8 @@
 
     def turn_over(chunk):
         a_each(chunk, lambda cp: cp.wait_recv())
-        at[chunk * 128:(chunk + 1) * 128, :] = ar[chunk].reshape(1024, 128).T
+        for h in range(*CHUNKS[chunk]):
+            at[h * 128:(h + 1) * 128, :] = ar[h].reshape(1024, 128).T
 
     def pairs(lo, hi):
         @pl.loop(0, 4)
@@ -224,7 +218,7 @@
                 send(1, 7 - k, q, True)
 
     def flush():
-        for chunk in range(4):
+        for chunk in range(3):
             a_each(chunk, lambda cp: cp.wait_send())
         for cp in sends:
             cp.wait_send()
@@ -245,12 +239,11 @@
     for q in range(Q):
         send(0, 8, q, False)
     turn_over(1)
-    turn_over(2)
     pairs(1, 3)
     for q in range(Q):
         send(1, 7, q, False)
     steps(1, 4)
-    turn_over(3)
+    turn_over(2)
     pairs(3, 4)
     for cp in zg[2:]:
         cp.wait_recv()
@@ -360,15 +353,12 @@
     return pl.pallas_call(
         kernel,
         out_shape=jax.ShapeDtypeStruct((4, 512, 256), BF16),
-        in_specs=[pl.BlockSpec(memory_space=pl.ANY)] * 6,
+        in_specs=[pl.BlockSpec(memory_space=pl.ANY)] * 3 + [pl.BlockSpec(memory_space=pltpu.SMEM)] * 3,
         out_specs=pl.BlockSpec(memory_space=pltpu.VMEM),
         scratch_shapes=[
             pltpu.VMEM((32, 64, 256), BF16),
             pltpu.VMEM((8, 128), F32),
             pltpu.VMEM((32, 128), F32),
-            pltpu.SMEM((4,), jnp.int32),
-            pltpu.SMEM((1,), jnp.int32),
-            pltpu.SMEM((1,), jnp.int32),
             pltpu.VMEM((4, 4, 4, 2, 32, 128), BF16),
             pltpu.VMEM((4, 32, 256), BF16),
             pltpu.VMEM((128, 256), F32),
@@ -385,7 +375,7 @@
             pltpu.SemaphoreType.DMA((COUNT,)),
         ],
         compiler_params=pltpu.CompilerParams(
-            collective_id=0, has_side_effects=True, vmem_limit_bytes=66 * 10**6
+            collective_id=0, has_side_effects=True, vmem_limit_bytes=55000000
         ),
         name="window",
     )(integrals, eps_occ.reshape(8, 128), eps_vir.reshape(32, 128), src_occ, occ_offset, vir_offset)

time: 91.7 us -> 91.2 us (level)
    unnamed x0 -> x6, local copies, waits for them, and re-layouts: none -> 1.36 us
    transpose x1, local copies, waits for them, and re-layouts: 3.01 us -> 1.78 us  [local(): return window(*args).transpose(1, 0, 2)]
where the time goes in v4:
time: 91.2 us; the launch traced here: 90.9 us
  Pallas kernels  86.4 us (95%)
  local copies, waits for them, and re-layouts  3.14 us (3%)
  between operations  1.34 us (1%)
    pallas_call x1, Pallas kernels, window(): pl.pallas_call(kernel, out_shape=jax.ShapeDtypeStruct((4, 512, 256), BF16...  86.4 us

profile of v4, /device:TPU:1, one launch (start us, length us, event | category | flops | bytes accessed | tf_op | source)
XLA Modules:
  0.0 90.9 jit_solution(7939732395932074967)
XLA Ops:
  0.0 0.0 copy-start.1
  1.3 0.0 copy-start.2
  1.3 0.0 copy-done.1
  1.3 0.6 copy-done.2
  2.0 0.0 copy-start
  2.0 0.7 copy-done
  2.7 86.4 %window.1 = bf16[4,512,256]{2,1,0:T(8,128)(2,1)S(1)} custom-call(bf16[32,64,256]{2,1,0:T(8,128)(2,1)} %a_hbm.1, f32[8,128]{1,0:T(8,128)S(1)} %bitcast.5, f32[32,128]{1,0:T(8,128)S(1)} %bitcast.4, s32[4]{0:T(128)S(1)} %copy-done.2, s32[1]{0:T(128)S(6)} %copy.8.oo_ref, s32[1]{0:T(128)S(6)} %copy.9.vo_ref), custom_call_target="tpu_custom_call" | custom-call | tf_op jit(solution)/shard_map/window/pallas_call | solution.py:353
  89.1 1.8 %copy.7 = bf16[512,4,256]{2,1,0:T(4,128)(2,1)} copy(bf16[512,4,256]{2,0,1:T(8,128)(2,1)S(1)} %bitcast.3) | data formatting | bytes 2097152 | tf_op jit(solution)/shard_map/transpose | solution.py:385
Async XLA Ops:
  0.0 1.3 %copy-start.1 = (f32[1024]{0:T(1024)S(1)}, f32[1024]{0:T(1024)}, u32[]{:S(2)}) copy-start(f32[1024]{0:T(1024)} %param.7) | copy-start | bytes 12292
  1.3 0.7 copy-start.2
  2.0 0.7 copy-start

commit v5 on v2

--- a/solution.py
+++ b/solution.py
@@ -9,7 +9,7 @@
 F32, BF16 = jnp.float32, jnp.bfloat16
 
 Q = 4
-SIZES = dict(A=96, SRC1=6, SRC2=6, FWD=8, ZG=4, XG=3, RING=16 * Q, AZ=3, AY=12, AR=8, AC=16, LOCAL=3)
+SIZES = dict(A=96, SRC1=6, SRC2=6, FWD=8, ZG=4, XG=3, RING=16 * Q, AZ=3, AY=12, AR=8, AC=16, BY=3, BZ=12, BC=16, LOCAL=3)
 SLOT, COUNT = {}, 0
 for _name, _size in SIZES.items():
     SLOT[_name] = COUNT
@@ -83,24 +83,6 @@
         pos = place(((j // 4) % 4 + 4 - zh) % 4)
         for tc in range(2):
             own_s[s, :, tc * 128:(tc + 1) * 128] = arel[j // 16, pos, j % 4, tc]
-
-    first_occ, first_vir = oo_ref[0], vo_ref[0]
-    e_occ = eo_ref[first_occ + (x * 4 + zh) * 4 + y]
-    e_src = eo_ref[first_occ + so_ref[zl]]
-    row, lane = first_vir // 128, first_vir % 128
-    window = jnp.concatenate(
-        [ev_ref[pl.ds(row, 1), :], ev_ref[pl.ds(row + 1, 1), :], ev_ref[pl.ds(jnp.minimum(row + 2, 31), 1), :]], axis=1
-    )
-
-    def column(count, offset):
-        at_lane = lax.broadcasted_iota(jnp.int32, (count, 384), 1)
-        wanted = lax.broadcasted_iota(jnp.int32, (count, 384), 0) + offset
-        return jnp.sum(jnp.where(at_lane == wanted, window, 0.0), axis=1, keepdims=True)
-
-    whole = column(256, lane)
-    diagonal = lax.broadcasted_iota(jnp.int32, (256, 256), 0) == lax.broadcasted_iota(jnp.int32, (256, 256), 1)
-    vir_b = jnp.sum(jnp.where(diagonal, whole, 0.0), axis=0, keepdims=True)
-    den[...] = column(128, lane + c * 128) + vir_b - e_occ - e_src
 
     pl.semaphore_wait(barrier, 38)
 
@@ -150,6 +132,24 @@
     fwd = [start(copy(v, v, SLOT["FWD"] + n, other)) for n, v in enumerate((vx, vy))]
     a_each(1, lambda cp: cp.start())
     a_each(2, lambda cp: cp.start())
+    first_occ, first_vir = oo_ref[0], vo_ref[0]
+    e_occ = eo_ref[first_occ + (x * 4 + zh) * 4 + y]
+    e_src = eo_ref[first_occ + so_ref[zl]]
+    row, lane = first_vir // 128, first_vir % 128
+    window = jnp.concatenate(
+        [ev_ref[pl.ds(row, 1), :], ev_ref[pl.ds(row + 1, 1), :], ev_ref[pl.ds(jnp.minimum(row + 2, 31), 1), :]], axis=1
+    )
+
+    def column(count, offset):
+        at_lane = lax.broadcasted_iota(jnp.int32, (count, 384), 1)
+        wanted = lax.broadcasted_iota(jnp.int32, (count, 384), 0) + offset
+        return jnp.sum(jnp.where(at_lane == wanted, window, 0.0), axis=1, keepdims=True)
+
+    whole = column(256, lane)
+    diagonal = lax.broadcasted_iota(jnp.int32, (256, 256), 0) == lax.broadcasted_iota(jnp.int32, (256, 256), 1)
+    vir_b = jnp.sum(jnp.where(diagonal, whole, 0.0), axis=0, keepdims=True)
+    den[...] = column(128, lane + c * 128) + vir_b - e_occ - e_src
+
     for n, j in enumerate(ORDER):
         for k, view in enumerate((sr.at[0:2, :, (y + 4 - j) % 4, c], sr.at[2:4, (x + 4 - j) % 4, :, c])):
             src2[2 * n + k].wait_recv()
@@ -240,28 +240,47 @@
         total = total + rb[0, 0, q].astype(F32)
         own[rows, :] = (total / den[rows, :]).astype(BF16)
 
+    most, rest = pl.ds(0, 96), pl.ds(96, 32)
+
     def block(j, m):
         return (y + 4 - m) % 4 * 4 + (zl + 4 - j) % 4
 
+    def group(j):
+        return device(x, y, zh * 4 + (zl + j) % 4, c)
+
     def to_z(j):
-        return copy(own, own, SLOT["AZ"] + j - 1, device(x, y, zh * 4 + (zl + j) % 4, c))
+        view = amp.at[block(0, 0), c, most]
+        return copy(view, view, SLOT["AZ"] + j - 1, group(j))
 
     def to_y(j, m):
-        view = amp.at[block(j, 0), c]
+        view = amp.at[block(j, 0), c, most]
         return copy(view, view, SLOT["AY"] + j * 3 + m - 1, device(x, ys[m], z, c))
 
     def relay(j, half):
-        view = amp.at[block(j, (1, 3)[half]), c, half * 64:(half + 1) * 64]
+        view = amp.at[block(j, (1, 3)[half]), c, pl.ds(half * 48, 48)]
         return copy(view, view, SLOT["AR"] + j * 2 + half, device(x, ys[(1, 3)[half]], z, c))
 
     def to_core(j, m):
-        view = amp.at[block(j, m), c]
+        view = amp.at[block(j, m), c, most]
         return copy(view, view, SLOT["AC"] + j * 4 + m, other)
+
+    def rest_y(m):
+        view = amp.at[block(0, 0), c, rest]
+        return copy(view, view, SLOT["BY"] + m - 1, device(x, ys[m], z, c))
+
+    def rest_z(j, m):
+        view = amp.at[block(0, m), c, rest]
+        return copy(view, view, SLOT["BZ"] + (j - 1) * 4 + m, group(j))
+
+    def rest_core(j, m):
+        view = amp.at[block(j, m), c, rest]
+        return copy(view, view, SLOT["BC"] + j * 4 + m, other)
 
     touched = set()
 
     def product(j, m, last=False):
         to_core(j, m).wait_recv()
+        rest_core(j, m).wait_recv()
         b = block(j, m)
         t, s = b // 4, b % 4
         lhs, rhs = sd[s].reshape(512, 256), amp[b].reshape(256, 256)
@@ -276,36 +295,57 @@
         else:
             dacc[t] = value
 
-    turn = (0, 1, 3, 2)
-    for j in turn:
-        if j:
-            to_z(j).wait_recv()
+    turn, near = (0, 1, 3, 2), (0, 1, 3)
+    for m in ORDER:
+        start(rest_y(m))
+    for k in (2, 1, 3):
+        start(to_z(k))
+    start(to_y(0, 1))
+    start(to_y(0, 3))
+    for k in (2, 1, 3):
+        start(rest_z(k, 0))
+    start(to_core(0, 0))
+    start(rest_core(0, 0))
+    for m in ORDER:
+        rest_y(m).wait_recv()
+        for k in (2, 1, 3):
+            start(rest_z(k, m))
+        start(rest_core(0, m))
+    for j in turn[1:]:
+        to_z(j).wait_recv()
         start(to_y(j, 1))
         start(to_y(j, 3))
-        if not j:
-            for k in ORDER:
-                start(to_z(k))
         start(to_core(j, 0))
     for cp in xg:
         cp.wait_recv()
-    for n, j in enumerate(turn):
+    for j in turn:
         for half, m in enumerate((1, 3)):
             to_y(j, m).wait_recv()
             start(relay(j, half))
             start(to_core(j, m))
-        if n:
-            for m in (0, 1, 3):
-                product(turn[n - 1], m)
-    for n, j in enumerate(turn):
+        if j == 3:
+            for m in near:
+                product(0, m)
+
+    def take(j):
         for half in range(2):
             relay(j, half).wait_recv()
         start(to_core(j, 2))
-        if n == 0:
-            for m in (0, 1, 3):
-                product(turn[3], m, True)
-        else:
-            product(turn[n - 1], 2)
-    product(turn[3], 2, True)
+
+    take(0)
+    for j in turn[1:]:
+        for m in turn:
+            rest_z(j, m).wait_recv()
+            start(rest_core(j, m))
+    for j in (1, 3):
+        take(j)
+        for m in near:
+            product(j, m)
+    take(2)
+    for m in near:
+        product(2, m, True)
+    for j in turn:
+        product(j, 2, j == 2)
     flush()
     flush_ring()
 

time: 88.8 us -> 90.4 us (1.018)
  Pallas kernels: 82.9 us -> 84.5 us
    pallas_call x1, Pallas kernels: 82.9 us -> 84.5 us  [window(): pl.pallas_call(kernel, out_shape=jax.ShapeDtypeStruct((4, 512, 256), BF16...]
where the time goes in v5:
time: 90.4 us; the launch traced here: 90.2 us
  Pallas kernels  84.5 us (93%)
  local copies, waits for them, and re-layouts  4.36 us (5%)
  between operations  1.34 us (1%)
    pallas_call x1, Pallas kernels, window(): pl.pallas_call(kernel, out_shape=jax.ShapeDtypeStruct((4, 512, 256), BF16...  84.5 us
    unnamed x8, local copies, waits for them, and re-layouts  2.58 us

profile of v5, /device:TPU:1, one launch (start us, length us, event | category | flops | bytes accessed | tf_op | source)
XLA Modules:
  0.0 90.2 jit_solution(2934822692537196680)
XLA Ops:
  0.0 0.0 copy-start.2
  1.3 0.0 copy-start.3
  1.3 0.0 copy-done.2
  1.3 0.6 copy-done.3
  2.0 0.0 copy-start
  2.0 1.2 %copy-done = bf16[32,64,256]{2,1,0:T(8,128)(2,1)S(1)} copy-done((bf16[32,64,256]{2,1,0:T(8,128)(2,1)S(1)}, bf16[32,64,256]{2,1,0:T(8,128)(2,1)}, u32[]{:S(2)}) %copy-start) | copy-done | bytes 1048600
  3.2 0.0 copy-start.1
  3.2 0.7 copy-done.1
  3.9 84.5 %window.1 = bf16[4,512,256]{2,1,0:T(8,128)(2,1)S(1)} custom-call(bf16[32,64,256]{2,1,0:T(8,128)(2,1)S(1)} %copy-done, f32[1024]{0:T(1024)S(1)} %copy-done.2, f32[32,128]{1,0:T(8,128)S(1)} %bitcast.3, s32[4]{0:T(128)S(1)} %copy-done.3, s32[1]{0:T(128)S(6)} %copy.8.oo_ref, s32[1]{0:T(128)S(6)} %copy.9.vo_ref), custom_call_target="tpu_custom_call" | custom-call | tf_op jit(solution)/shard_map/window/pallas_call | solution.py:355
  88.4 1.8 %copy.7 = bf16[512,4,256]{2,1,0:T(4,128)(2,1)} copy(bf16[512,4,256]{2,0,1:T(8,128)(2,1)S(1)} %bitcast.2) | data formatting | bytes 2097152 | tf_op jit(solution)/shard_map/transpose | solution.py:384
Async XLA Ops:
  0.0 1.3 %copy-start.2 = (f32[1024]{0:T(1024)S(1)}, f32[1024]{0:T(1024)}, u32[]{:S(2)}) copy-start(f32[1024]{0:T(1024)} %eo_ref.1) | copy-start | bytes 12292
  1.3 0.7 copy-start.3
  2.0 1.2 %copy-start = (bf16[32,64,256]{2,1,0:T(8,128)(2,1)S(1)}, bf16[32,64,256]{2,1,0:T(8,128)(2,1)}, u32[]{:S(2)}) copy-start(bf16[32,64,256]{2,1,0:T(8,128)(2,1)} %a_ref.1) | copy-start | bytes 3145732
  3.2 0.7 copy-start.1

commit v6 on v5

--- a/solution.py
+++ b/solution.py
@@ -83,6 +83,24 @@
         pos = place(((j // 4) % 4 + 4 - zh) % 4)
         for tc in range(2):
             own_s[s, :, tc * 128:(tc + 1) * 128] = arel[j // 16, pos, j % 4, tc]
+
+    first_occ, first_vir = oo_ref[0], vo_ref[0]
+    e_occ = eo_ref[first_occ + (x * 4 + zh) * 4 + y]
+    e_src = eo_ref[first_occ + so_ref[zl]]
+    row, lane = first_vir // 128, first_vir % 128
+    window = jnp.concatenate(
+        [ev_ref[pl.ds(row, 1), :], ev_ref[pl.ds(row + 1, 1), :], ev_ref[pl.ds(jnp.minimum(row + 2, 31), 1), :]], axis=1
+    )
+
+    def column(count, offset):
+        at_lane = lax.broadcasted_iota(jnp.int32, (count, 384), 1)
+        wanted = lax.broadcasted_iota(jnp.int32, (count, 384), 0) + offset
+        return jnp.sum(jnp.where(at_lane == wanted, window, 0.0), axis=1, keepdims=True)
+
+    whole = column(256, lane)
+    diagonal = lax.broadcasted_iota(jnp.int32, (256, 256), 0) == lax.broadcasted_iota(jnp.int32, (256, 256), 1)
+    vir_b = jnp.sum(jnp.where(diagonal, whole, 0.0), axis=0, keepdims=True)
+    den[...] = column(128, lane + c * 128) + vir_b - e_occ - e_src
 
     pl.semaphore_wait(barrier, 38)
 
@@ -132,24 +150,6 @@
     fwd = [start(copy(v, v, SLOT["FWD"] + n, other)) for n, v in enumerate((vx, vy))]
     a_each(1, lambda cp: cp.start())
     a_each(2, lambda cp: cp.start())
-    first_occ, first_vir = oo_ref[0], vo_ref[0]
-    e_occ = eo_ref[first_occ + (x * 4 + zh) * 4 + y]
-    e_src = eo_ref[first_occ + so_ref[zl]]
-    row, lane = first_vir // 128, first_vir % 128
-    window = jnp.concatenate(
-        [ev_ref[pl.ds(row, 1), :], ev_ref[pl.ds(row + 1, 1), :], ev_ref[pl.ds(jnp.minimum(row + 2, 31), 1), :]], axis=1
-    )
-
-    def column(count, offset):
-        at_lane = lax.broadcasted_iota(jnp.int32, (count, 384), 1)
-        wanted = lax.broadcasted_iota(jnp.int32, (count, 384), 0) + offset
-        return jnp.sum(jnp.where(at_lane == wanted, window, 0.0), axis=1, keepdims=True)
-
-    whole = column(256, lane)
-    diagonal = lax.broadcasted_iota(jnp.int32, (256, 256), 0) == lax.broadcasted_iota(jnp.int32, (256, 256), 1)
-    vir_b = jnp.sum(jnp.where(diagonal, whole, 0.0), axis=0, keepdims=True)
-    den[...] = column(128, lane + c * 128) + vir_b - e_occ - e_src
-
     for n, j in enumerate(ORDER):
         for k, view in enumerate((sr.at[0:2, :, (y + 4 - j) % 4, c], sr.at[2:4, (x + 4 - j) % 4, :, c])):
             src2[2 * n + k].wait_recv()

time: 90.4 us -> 90.4 us (level)
  no operation moved by 1% of the time
where the time goes in v6:
time: 90.4 us; the launch traced here: 90.2 us
  Pallas kernels  84.5 us (93%)
  local copies, waits for them, and re-layouts  4.36 us (5%)
  between operations  1.34 us (1%)
    pallas_call x1, Pallas kernels, window(): pl.pallas_call(kernel, out_shape=jax.ShapeDtypeStruct((4, 512, 256), BF16...  84.5 us
    unnamed x8, local copies, waits for them, and re-layouts  2.58 us

profile of v6, /device:TPU:1, one launch (start us, length us, event | category | flops | bytes accessed | tf_op | source)
XLA Modules:
  0.0 90.2 jit_solution(2887077261939123289)
XLA Ops:
  0.0 0.0 copy-start.2
  1.3 0.0 copy-start.3
  1.3 0.0 copy-done.2
  1.3 0.6 copy-done.3
  2.0 0.0 copy-start
  2.0 1.2 %copy-done = bf16[32,64,256]{2,1,0:T(8,128)(2,1)S(1)} copy-done((bf16[32,64,256]{2,1,0:T(8,128)(2,1)S(1)}, bf16[32,64,256]{2,1,0:T(8,128)(2,1)}, u32[]{:S(2)}) %copy-start) | copy-done | bytes 1048600
  3.2 0.0 copy-start.1
  3.2 0.7 copy-done.1
  3.9 84.5 %window.1 = bf16[4,512,256]{2,1,0:T(8,128)(2,1)S(1)} custom-call(bf16[32,64,256]{2,1,0:T(8,128)(2,1)S(1)} %copy-done, f32[1024]{0:T(1024)S(1)} %copy-done.2, f32[32,128]{1,0:T(8,128)S(1)} %bitcast.3, s32[4]{0:T(128)S(1)} %copy-done.3, s32[1]{0:T(128)S(6)} %copy.8.oo_ref, s32[1]{0:T(128)S(6)} %copy.9.vo_ref), custom_call_target="tpu_custom_call" | custom-call | tf_op jit(solution)/shard_map/window/pallas_call | solution.py:355
  88.4 1.8 %copy.7 = bf16[512,4,256]{2,1,0:T(4,128)(2,1)} copy(bf16[512,4,256]{2,0,1:T(8,128)(2,1)S(1)} %bitcast.2) | data formatting | bytes 2097152 | tf_op jit(solution)/shard_map/transpose | solution.py:384
Async XLA Ops:
  0.0 1.3 %copy-start.2 = (f32[1024]{0:T(1024)S(1)}, f32[1024]{0:T(1024)}, u32[]{:S(2)}) copy-start(f32[1024]{0:T(1024)} %eo_ref.1) | copy-start | bytes 12292
  1.3 0.7 copy-start.3
  2.0 1.2 %copy-start = (bf16[32,64,256]{2,1,0:T(8,128)(2,1)S(1)}, bf16[32,64,256]{2,1,0:T(8,128)(2,1)}, u32[]{:S(2)}) copy-start(bf16[32,64,256]{2,1,0:T(8,128)(2,1)} %a_ref.1) | copy-start | bytes 3145732
  3.2 0.7 copy-start.1
